TPU v7x, 32 devices: a whole 2x2x4 slice. The times are simulated.
32 devices in a mesh: parts: 2 (over y), db: 4 (over z), blk: 4 (over x, core).
Axes of the slice: x: 2, y: 2, z: 4, core: 2. Of those that a mesh axis runs over, the one named last changes fastest.
Arguments:
- queries: bfloat16 [8192, 768], P(('parts', 'db', 'blk')), parts along dimension 0, may hold values from -6 to 6
- projection: bfloat16 [768, 768], replicated, may hold values from -0.21875 to 0.21875
- vectors: bfloat16 [768, 32768], P(None, ('parts', 'db', 'blk')), parts along dimension 1, may hold values from -0.21875 to 0.21875
- bins: int32 [32768], P(('parts', 'db', 'blk')), parts along dimension 0, may hold values from 0 to 127, as said below
- routes: int32 [8192, 1], P(('parts', 'db', 'blk')), parts along dimension 0, may hold values from 0 to 3; in each aligned block of 256 rows (0 to 255, 256 to 511, ...) at most 128 rows name the same one
Outputs:
- best: float32 [8192, 128], P(('parts', 'db', 'blk')), parts along dimension 0
There are 2 independent parts, one for each index of `parts`. A program takes and returns all parts, laid end to end along the dimension named above; an argument that names none is the same for every part. Nothing has to cross between parts.
Inputs may be any that keep to these rules, and one draw needn't show every extreme that they name: Within every aligned block of 1024 entries each of the 128 bins occurs exactly 1024 // 128 times. `routes`: within every aligned block of 256 rows no group is named by more than 128 rows; in every draw some block names some group exactly 128 times.
All inputs are finite; a program needn't handle non-finite values.
Results may differ from a plain program's by a relative error of at most 0.0014.
Values may be sent and summed in bfloat16 or wider, within the bound.
A program may use at most 64 MiB of HBM per device.

v0:
```python
import functools

import jax
import jax.numpy as jnp
from jax import lax
from jax.experimental import pallas as pl
from jax.experimental.pallas import tpu as pltpu
from jax.sharding import PartitionSpec as P

BINS = 128
TILE = 256
logit_scale = 10.0
MESH = pl.DeviceIdType.MESH


CODE_SCALE = 2.0 ** 26


def encode(score):
    scaled = score * CODE_SCALE
    square = scaled * scaled
    fourth = square * square
    return jnp.where(score < 0, -fourth, fourth)


def decode(code):
    root = jnp.sqrt(jnp.sqrt(jnp.abs(code))) * (1.0 / CODE_SCALE)
    return jnp.where(code < 0, -root, root)


def kernel(
    G, NB, sizes,
    q_hbm, p_hbm, v_hbm, b_hbm, r_hbm,
    out_ref,
    q_ref, p_ref, raw, bins_ref, routes_ref, slab, chooser, outgoing, rows, own, xout, xin, back, ans,
    load_sem, z_ss, z_rs, x_ss, x_rs, s_ss, s_rs, xb_ss, xb_rs, zb_ss, zb_rs,
):
    H = NB // 2
    C = len(sizes)
    firsts = [sum(sizes[:c]) for c in range(C)]
    n, depth = q_ref.shape
    width = raw.shape[1]
    tiles = width // TILE
    f32, bf16 = jnp.float32, jnp.bfloat16
    d = lax.axis_index("db")
    k = lax.axis_index("blk")

    loads = [
        pltpu.make_async_copy(r_hbm, routes_ref, load_sem.at[0]),
        pltpu.make_async_copy(q_hbm, q_ref, load_sem.at[1]),
        pltpu.make_async_copy(p_hbm, p_ref, load_sem.at[2]),
        pltpu.make_async_copy(b_hbm, bins_ref, load_sem.at[3]),
        pltpu.make_async_copy(v_hbm, raw, load_sem.at[4]),
    ]
    for load in loads:
        load.start()

    barrier = pltpu.get_barrier_semaphore()
    for o in range(1, G):
        pl.semaphore_signal(barrier, inc=1, device_id={"db": d ^ o}, device_id_type=MESH)
    for h in range(1, H):
        pl.semaphore_signal(barrier, inc=1, device_id={"blk": k ^ (2 * h)}, device_id_type=MESH)
    pl.semaphore_signal(barrier, inc=1, device_id={"blk": k ^ 1}, device_id_type=MESH)

    def block(c, h, o):
        return rows.at[pl.ds(H * G * firsts[c] + (h * G + o) * sizes[c], sizes[c])]

    def part(c, o):
        return pl.ds(G * firsts[c] + o * sizes[c], sizes[c])

    def whole(c):
        return pl.ds(G * firsts[c], G * sizes[c])

    def z_copy(c, o):
        return pltpu.make_async_remote_copy(
            src_ref=outgoing.at[part(c, o)], dst_ref=block(c, 0, o),
            send_sem=z_ss.at[c, o], recv_sem=z_rs.at[c, o],
            device_id={"db": d ^ o}, device_id_type=MESH)

    def x_copy(c, h, o, step):
        return pltpu.make_async_remote_copy(
            src_ref=block(c, h, o), dst_ref=block(c, h + step, o),
            send_sem=x_ss.at[c, h + step, o], recv_sem=x_rs.at[c, h + step, o],
            device_id={"blk": k ^ (2 * step)}, device_id_type=MESH)

    def s_copy(t):
        return pltpu.make_async_remote_copy(
            src_ref=slab.at[0, t], dst_ref=slab.at[1, t],
            send_sem=s_ss.at[t], recv_sem=s_rs.at[t],
            device_id={"blk": k ^ 1}, device_id_type=MESH)

    def xb_copy(c, h):
        return pltpu.make_async_remote_copy(
            src_ref=xout.at[h - 1, whole(c)], dst_ref=xin.at[h - 1, whole(c)],
            send_sem=xb_ss.at[c, h], recv_sem=xb_rs.at[c, h],
            device_id={"blk": k ^ (2 * h)}, device_id_type=MESH)

    def zb_copy(c, o):
        return pltpu.make_async_remote_copy(
            src_ref=back.at[part(c, o)], dst_ref=ans.at[part(c, o)],
            send_sem=zb_ss.at[c, o], recv_sem=zb_rs.at[c, o],
            device_id={"db": d ^ o}, device_id_type=MESH)

    started = []

    def start(copy):
        copy.start()
        started.append(copy)

    loads[0].wait()
    target = routes_ref[...]
    pad = max(8, G)
    hot = jnp.where(lax.broadcasted_iota(jnp.int32, (pad, n), 0) == target, 1.0, 0.0)
    before = jnp.where(
        lax.broadcasted_iota(jnp.int32, (n, n), 0) < lax.broadcasted_iota(jnp.int32, (n, n), 1),
        1.0, 0.0).astype(bf16)
    earlier = jnp.dot(hot.astype(bf16), before, preferred_element_type=f32)
    slot = jnp.sum(hot * earlier, axis=0, keepdims=True).astype(jnp.int32)
    position = (target ^ d) * sizes[0] + slot
    for c in range(1, C):
        position = jnp.where(
            slot < firsts[c], position,
            G * firsts[c] + (target ^ d) * sizes[c] + slot - firsts[c])

    loads[1].wait()
    loads[2].wait()
    projected = jnp.dot(q_ref[...], p_ref[...], preferred_element_type=f32)
    normed = (
        projected * lax.rsqrt(jnp.sum(projected * projected, axis=1, keepdims=True) + 1e-06)
    ).astype(bf16)

    pl.semaphore_wait(barrier, G - 1 + H)

    for c in range(C):
        pick = jnp.where(
            lax.broadcasted_iota(jnp.int32, (G * sizes[c], n), 0) + G * firsts[c] == position,
            1.0, 0.0).astype(bf16)
        chooser[whole(c), :] = pick
        chosen = jnp.dot(pick, normed, preferred_element_type=f32).astype(bf16)
        outgoing[whole(c)] = chosen
        rows[pl.ds(H * G * firsts[c], sizes[c])] = chosen[:sizes[c]]
        for o in range(1, G):
            start(z_copy(c, o))
        if H > 1:
            start(x_copy(c, 0, 0, 1))

    loads[3].wait()
    loads[4].wait()
    bins = bins_ref[...]
    inner = jnp.where(
        lax.broadcasted_iota(jnp.int32, (BINS, BINS), 0)
        < lax.broadcasted_iota(jnp.int32, (BINS, BINS), 1), 1.0, 0.0).astype(bf16)
    run = jnp.zeros((BINS, 1), f32)
    places = []
    for s in range(width // BINS):
        mine = bins[:, s * BINS:(s + 1) * BINS]
        hot = jnp.where(lax.broadcasted_iota(jnp.int32, (BINS, BINS), 0) == mine, 1.0, 0.0)
        earlier = jnp.dot(hot.astype(bf16), inner, preferred_element_type=f32) + run
        rank = jnp.sum(hot * earlier, axis=0, keepdims=True).astype(jnp.int32)
        places.append(rank * BINS + mine)
        run = run + jnp.sum(hot, axis=1, keepdims=True)
    place = jnp.concatenate(places, axis=1)
    for t in range(tiles):
        move = jnp.where(
            lax.broadcasted_iota(jnp.int32, (TILE, width), 0) + t * TILE == place, 1.0, 0.0
        ).astype(bf16)
        slab[0, t] = lax.dot_general(
            raw[...], move, (((1,), (1,)), ((), ())), preferred_element_type=f32).astype(bf16)
        start(s_copy(t))

    def relay(c):
        for o in range(1, G):
            z_copy(c, o).wait_recv()
            if H > 1:
                start(x_copy(c, 0, o, 1))
        step = 2
        while step < H:
            for o in range(G):
                for h in range(step):
                    if h >= step // 2:
                        x_copy(c, h - step // 2, o, step // 2).wait_recv()
                    start(x_copy(c, h, o, step))
            step *= 2

    def score(c):
        half = H // 2
        for h in range(half, H):
            if h:
                for o in range(G):
                    x_copy(c, h - half, o, half).wait_recv()
        if c == 0:
            for t in range(tiles):
                s_copy(t).wait_recv()
        count = G * sizes[c]
        base = H * G * firsts[c]

        for h0 in range(H):
            if H > 2 or h0 == 0:
                span = count if H > 2 else H * count
                x = rows[pl.ds(base + h0 * count, span)]
                best = None
                for side in range(2):
                    for t in range(tiles):
                        sc = jnp.dot(x, slab[side, t], preferred_element_type=f32)
                        top = jnp.maximum(sc[:, :BINS], sc[:, BINS:])
                        best = top if best is None else jnp.maximum(best, top)
                best = encode(best).astype(bf16)
                for i in range(span // count):
                    h = h0 + i
                    piece = best[i * count:(i + 1) * count]
                    if h == 0:
                        own[whole(c)] = piece
                    else:
                        xout[h - 1, whole(c)] = piece
                        start(xb_copy(c, h))

    def combine(c):
        total = own[whole(c)]
        for h in range(1, H):
            xb_copy(c, h).wait_recv()
            total = jnp.maximum(total, xin[h - 1, whole(c)])
        back[whole(c)] = total
        ans[part(c, 0)] = total[:sizes[c]]
        for o in range(G - 1, 0, -1):
            start(zb_copy(c, o))

    for step in range(C + 2):
        if step < C:
            relay(step)
        if 0 <= step - 1 < C:
            score(step - 1)
        if 0 <= step - 2 < C:
            combine(step - 2)

    total = None
    for c in range(C):
        for o in range(1, G):
            zb_copy(c, o).wait_recv()
        got = lax.dot_general(
            chooser[whole(c), :], ans[whole(c)], (((0,), (0,)), ((), ())),
            preferred_element_type=f32)
        total = got if total is None else total + got
    out_ref[...] = decode(total)
    for copy in started:
        copy.wait_send()


def per_device(queries, projection, vectors, bins, routes):
    G, NB = lax.axis_size("db"), lax.axis_size("blk")
    n, depth = queries.shape
    width = vectors.shape[1]
    cap = 2 * n // G
    unit = cap // 8
    sizes = [3 * unit, 3 * unit, 2 * unit] if cap % 128 == 0 else [cap]
    C = len(sizes)
    H = NB // 2
    tiles = width // TILE
    f32, bf16 = jnp.float32, jnp.bfloat16
    hbm = pl.BlockSpec(memory_space=pltpu.HBM)
    vmem = pl.BlockSpec(memory_space=pltpu.VMEM)
    dma = pltpu.SemaphoreType.DMA
    out = pl.pallas_call(
        functools.partial(kernel, G, NB, tuple(sizes)),
        out_shape=jax.ShapeDtypeStruct((n, BINS), f32),
        in_specs=[hbm] * 5,
        out_specs=vmem,
        scratch_shapes=[
            pltpu.VMEM((n, depth), bf16),
            pltpu.VMEM(projection.shape, bf16),
            pltpu.VMEM((depth, width), bf16),
            pltpu.VMEM((1, width), jnp.int32),
            pltpu.VMEM((1, n), jnp.int32),
            pltpu.VMEM((2, tiles, depth, TILE), bf16),
            pltpu.VMEM((G * cap, n), bf16),
            pltpu.VMEM((G * cap, depth), bf16),
            pltpu.VMEM((H * G * cap, depth), bf16),
            pltpu.VMEM((G * cap, BINS), bf16),
            pltpu.VMEM((max(1, H - 1), G * cap, BINS), bf16),
            pltpu.VMEM((max(1, H - 1), G * cap, BINS), bf16),
            pltpu.VMEM((G * cap, BINS), bf16),
            pltpu.VMEM((G * cap, BINS), bf16),
            dma((5,)),
            dma((C, G)), dma((C, G)),
            dma((C, H, G)), dma((C, H, G)),
            dma((tiles,)), dma((tiles,)),
            dma((C, H)), dma((C, H)),
            dma((C, G)), dma((C, G)),
        ],
        compiler_params=pltpu.CompilerParams(
            collective_id=0, has_side_effects=True, vmem_limit_bytes=63 * 1024 * 1024),
    )(queries, projection, vectors, bins.reshape(1, -1), routes.reshape(1, -1))
    return logit_scale * out


def solution(mesh):
    in_specs = (
        P(("parts", "db", "blk"), None),
        P(),
        P(None, ("parts", "db", "blk")),
        P(("parts", "db", "blk")),
        P(("parts", "db", "blk"), None),
    )
    out_specs = P(("parts", "db", "blk"), None)
    return jax.shard_map(
        per_device, mesh=mesh, in_specs=in_specs, out_specs=out_specs, check_vma=False
    )
```

profile of v0, /device:TPU:0, one launch (start us, length us, event | category | flops | bytes accessed | tf_op | source)
XLA Modules:
  0.0 39.7 jit_solution(5850985094446855172)
XLA Ops:
  0.0 38.1 %shard_map.55 = f32[256,128]{1,0:T(8,128)} custom-call(bf16[256,768]{1,0:T(8,128)(2,1)} %q_hbm.1, bf16[768,768]{1,0:T(8,128)(2,1)} %p_hbm.1, bf16[768,1024]{1,0:T(8,128)(2,1)} %v_hbm.1, s32[1,1024]{1,0:T(1,128)} %bitcast.2, s32[1,256]{1,0:T(1,128)} %bitcast.3), custom_call_target="tpu_custom_call" | custom-call | tf_op jit(solution)/shard_map/pallas_call | solution.py:262
  38.1 1.6 %broadcast_multiply_fusion = f32[256,128]{1,0:T(8,128)} fusion(f32[256,128]{1,0:T(8,128)} %shard_map.55), kind=kLoop, calls=%fused_computation | loop fusion | flops 32768 | bytes 262144 | tf_op jit(solution)/shard_map/mul | solution.py:292
where the time goes:
time: 39.8 us; the launch traced here: 39.7 us
  Pallas kernels  38.1 us (96%)
  other arithmetic  1.57 us (4%)
    pallas_call x1, Pallas kernels, per_device(): pl.pallas_call(functools.partial(kernel, G, NB, tuple(sizes)), out_shape=...  38.1 us
    mul x1, other arithmetic, per_device(): return logit_scale * out  1.57 us

commit v1 on v0

v1 whole, which is shorter than its diff:
```python
import functools

import jax
import jax.numpy as jnp
from jax import lax
from jax.experimental import pallas as pl
from jax.experimental.pallas import tpu as pltpu
from jax.sharding import PartitionSpec as P

BINS = 128
TILE = 256
logit_scale = 10.0
MESH = pl.DeviceIdType.MESH


CODE_SCALE = 2.0 ** 26


def encode(score):
    scaled = score * CODE_SCALE
    square = scaled * scaled
    fourth = square * square
    return jnp.where(score < 0, -fourth, fourth)


def decode(code):
    root = jnp.sqrt(jnp.sqrt(jnp.abs(code))) * (1.0 / CODE_SCALE)
    return jnp.where(code < 0, -root, root)


def kernel(
    G, NB, cap, sizes,
    q_hbm, p_hbm, v_hbm, b_hbm, r_hbm,
    out_ref,
    q_ref, p_ref, raw, bins_ref, routes_ref, slab, chooser, outgoing, rows, own, xout, xin, back, ans,
    load_sem, z_rs, x_rs, s_rs, xb_rs, zb_rs, sent,
):
    H = NB // 2
    C = len(sizes)
    n, depth = q_ref.shape
    width = raw.shape[1]
    tiles = width // TILE
    f32, bf16 = jnp.float32, jnp.bfloat16
    d = lax.axis_index("db")
    k = lax.axis_index("blk")

    load_r = pltpu.make_async_copy(r_hbm, routes_ref, load_sem.at[0])
    load_q = pltpu.make_async_copy(q_hbm, q_ref, load_sem.at[1])
    load_p = pltpu.make_async_copy(p_hbm, p_ref, load_sem.at[2])
    load_b = pltpu.make_async_copy(b_hbm, bins_ref, load_sem.at[3])
    load_v = pltpu.make_async_copy(v_hbm, raw, load_sem.at[4])

    barrier = pltpu.get_barrier_semaphore()
    for o in range(G - 1, 0, -1):
        pl.semaphore_signal(barrier, inc=1, device_id={"db": d ^ o}, device_id_type=MESH)
    for h in range(1, H):
        pl.semaphore_signal(barrier, inc=1, device_id={"blk": k ^ (2 * h)}, device_id_type=MESH)
    pl.semaphore_signal(barrier, inc=1, device_id={"blk": k ^ 1}, device_id_type=MESH)
    for load in (load_r, load_q, load_p, load_b):
        load.start()

    if G == 4 and C == 4:
        inner = ((d + 1) // 2) % 2
        outer_order = [(2, 0), (2, 1), (2, 2), *((1, c) for c in range(C)), *((3, c) for c in range(C)), (2, 3)]
        inner_order = [(o, c) for o in (1, 2, 3) for c in range(C)]

        def either(a, b):
            return a if a == b else a + inner * (b - a)

        order = [(either(a, i), either(b, j)) for (a, b), (i, j) in zip(outer_order, inner_order)]
        units = [[(0, c) for c in range(C)], order[:4], order[4:8], order[8:10], order[10:]]
    else:
        units = [[(o, c) for o in range(G) for c in range(C)]]
    rank = sizes[0]

    def fixed(start, multiple=16):
        return start if isinstance(start, int) else pl.multiple_of(start, multiple)

    def slots(o, c):
        return pl.ds(fixed(o * cap + c * rank), rank)

    def group(o):
        return pl.ds(fixed(o * cap), cap)

    def block(o, c, h=0, many=1):
        return pl.ds(fixed(o * (H * cap) + (c * H + h) * rank), many * rank)

    def span(u):
        return pl.ds(sum(len(v) for v in units[:u]) * rank, len(units[u]) * rank)

    def z_copy(o, c):
        return pltpu.make_async_remote_copy(
            src_ref=outgoing.at[slots(o, c)], dst_ref=rows.at[block(o, c)],
            send_sem=sent.at[0], recv_sem=z_rs.at[c, o - 1],
            device_id={"db": d ^ o}, device_id_type=MESH)

    def x_copy(u, o, c, h, step):
        return pltpu.make_async_remote_copy(
            src_ref=rows.at[block(o, c, h)], dst_ref=rows.at[block(o, c, h + step)],
            send_sem=sent.at[1], recv_sem=x_rs.at[u, h + step - 1],
            device_id={"blk": k ^ (2 * step)}, device_id_type=MESH)

    def s_copy(t):
        return pltpu.make_async_remote_copy(
            src_ref=slab.at[0, t], dst_ref=slab.at[1, t],
            send_sem=sent.at[2], recv_sem=s_rs.at[t],
            device_id={"blk": k ^ 1}, device_id_type=MESH)

    def xb_copy(u, h):
        return pltpu.make_async_remote_copy(
            src_ref=xout.at[h - 1, span(u)], dst_ref=xin.at[h - 1, span(u)],
            send_sem=sent.at[3], recv_sem=xb_rs.at[u, h - 1],
            device_id={"blk": k ^ (2 * h)}, device_id_type=MESH)

    def zb_copy(o, c):
        return pltpu.make_async_remote_copy(
            src_ref=back.at[slots(o, c)], dst_ref=ans.at[slots(o, c)],
            send_sem=sent.at[4], recv_sem=zb_rs.at[o - 1],
            device_id={"db": d ^ o}, device_id_type=MESH)

    def await_bytes(ref, sem):
        pltpu.make_async_copy(ref, ref, sem).wait()

    def local(o):
        return isinstance(o, int) and o == 0

    load_r.wait()
    target = routes_ref[...]
    pad = max(8, G)
    hot = jnp.where(lax.broadcasted_iota(jnp.int32, (pad, n), 0) == target, 1.0, 0.0)
    before = jnp.where(
        lax.broadcasted_iota(jnp.int32, (n, n), 0) < lax.broadcasted_iota(jnp.int32, (n, n), 1),
        1.0, 0.0).astype(bf16)
    earlier = jnp.dot(hot.astype(bf16), before, preferred_element_type=f32)
    slot = jnp.sum(hot * earlier, axis=0, keepdims=True).astype(jnp.int32)
    position = (target ^ d) * cap + slot

    load_q.wait()
    load_v.start()
    load_p.wait()
    projected = jnp.dot(q_ref[...], p_ref[...], preferred_element_type=f32)
    normed = (
        projected * lax.rsqrt(jnp.sum(projected * projected, axis=1, keepdims=True) + 1e-06)
    ).astype(bf16)

    pl.semaphore_wait(barrier, G - 1 + H)

    def choose(o):
        pick = jnp.where(
            lax.broadcasted_iota(jnp.int32, (cap, n), 0) + o * cap == position, 1.0, 0.0
        ).astype(bf16)
        chooser[group(o), :] = pick
        chosen = jnp.dot(pick, normed, preferred_element_type=f32).astype(bf16)
        if o:
            outgoing[group(o), :] = chosen
            for c in range(C):
                z_copy(o, c).start()
        else:
            for c in range(C):
                rows[block(0, c)] = chosen[c * rank:(c + 1) * rank]
                if H > 1:
                    x_copy(0, 0, c, 0, 1).start()

    for o in [1, 2, 0, *range(3, G)] if G > 2 else range(G):
        choose(o)

    def relay(u, i):
        o, c = units[u][i]
        z_copy(o, c).wait_recv()
        if H > 1:
            x_copy(u, o, c, 0, 1).start()

    load_b.wait()
    load_v.wait()
    bins = bins_ref[...]
    inner_mask = jnp.where(
        lax.broadcasted_iota(jnp.int32, (BINS, BINS), 0)
        < lax.broadcasted_iota(jnp.int32, (BINS, BINS), 1), 1.0, 0.0).astype(bf16)
    run = jnp.zeros((BINS, 1), f32)
    places = []
    for s in range(width // BINS):
        mine = bins[:, s * BINS:(s + 1) * BINS]
        hot = jnp.where(lax.broadcasted_iota(jnp.int32, (BINS, BINS), 0) == mine, 1.0, 0.0)
        earlier = jnp.dot(hot.astype(bf16), inner_mask, preferred_element_type=f32) + run
        turn = jnp.sum(hot * earlier, axis=0, keepdims=True).astype(jnp.int32)
        places.append(turn * BINS + mine)
        run = run + jnp.sum(hot, axis=1, keepdims=True)
    place = jnp.concatenate(places, axis=1)
    for t in range(tiles):
        move = jnp.where(
            lax.broadcasted_iota(jnp.int32, (TILE, width), 0) + t * TILE == place, 1.0, 0.0
        ).astype(bf16)
        slab[0, t] = lax.dot_general(
            raw[...], move, (((1,), (1,)), ((), ())), preferred_element_type=f32).astype(bf16)
        s_copy(t).start()

    def whole(u):
        return rows.at[pl.ds(0, len(units[u]) * rank)]

    def spread(u):
        step = 2
        while step < H:
            for h in range(step):
                if h >= step // 2:
                    await_bytes(whole(u), x_rs.at[u, h - 1])
                for o, c in units[u]:
                    x_copy(u, o, c, h, step).start()
            step *= 2

    met = [False]

    def score(u):
        spread(u)
        for h in range(max(1, H // 2), H):
            await_bytes(whole(u), x_rs.at[u, h - 1])
        first = not met[0]
        met[0] = True
        x = jnp.concatenate([rows[block(o, c, 0, H)] for o, c in units[u]], axis=0)
        best = None
        for side in range(2):
            for t in range(tiles):
                if first and side == 1:
                    s_copy(t).wait_recv()
                sc = jnp.dot(x, slab[side, t], preferred_element_type=f32)
                top = jnp.maximum(sc[:, :BINS], sc[:, BINS:])
                best = top if best is None else jnp.maximum(best, top)
        best = encode(best).astype(bf16)
        to = sum(len(v) for v in units[:u]) * rank
        for i in range(len(units[u])):
            for h in range(H):
                piece = best[(i * H + h) * rank:(i * H + h + 1) * rank]
                if h == 0:
                    own[pl.ds(to + i * rank, rank)] = piece
                else:
                    xout[h - 1, pl.ds(to + i * rank, rank)] = piece
        for h in range(1, H):
            xb_copy(u, h).start()

    def combine(u):
        total = own[span(u)]
        for h in range(1, H):
            xb_copy(u, h).wait_recv()
            total = jnp.maximum(total, xin[h - 1, span(u)])
        for i, (o, c) in enumerate(units[u]):
            piece = total[i * rank:(i + 1) * rank]
            if isinstance(o, int) and o == 0:
                ans[slots(0, c)] = piece
            else:
                back[slots(o, c)] = piece
                zb_copy(o, c).start()

    def unpick(o):
        if o:
            await_bytes(ans.at[group(o)], zb_rs.at[o - 1])
        return lax.dot_general(
            chooser[group(o), :], ans[group(o)], (((0,), (0,)), ((), ())), preferred_element_type=f32)

    if len(units) > 1:
        for i in range(4):
            relay(1, i)
        relay(2, 0)
        relay(2, 1)
        score(0)
        relay(2, 2)
        relay(2, 3)
        score(1)
        combine(0)
        relay(3, 0)
        relay(3, 1)
        relay(4, 0)
        relay(4, 1)
        combine(1)
        score(2)
        score(3)
        combine(2)
        score(4)
        combine(3)
        combine(4)
    else:
        for i, (o, c) in enumerate(units[0]):
            if o:
                relay(0, i)
        score(0)
        combine(0)
    total = unpick(0)
    for o in range(1, G):
        total = total + unpick(o)
    out_ref[...] = total.astype(bf16)

    away = pl.ds(cap, (G - 1) * cap)
    await_bytes(outgoing.at[away], sent.at[0])
    if H > 1:
        await_bytes(rows.at[pl.ds(0, (H - 1) * G * cap)], sent.at[1])
        await_bytes(xout, sent.at[3])
    await_bytes(slab.at[0], sent.at[2])
    await_bytes(back.at[away], sent.at[4])


def per_device(queries, projection, vectors, bins, routes):
    G, NB = lax.axis_size("db"), lax.axis_size("blk")
    n, depth = queries.shape
    width = vectors.shape[1]
    cap = 2 * n // G
    sizes = [cap // 4] * 4 if cap % 64 == 0 else [cap]
    C = len(sizes)
    H = NB // 2
    tiles = width // TILE
    units = 5 if G == 4 and C == 4 else 1
    f32, bf16 = jnp.float32, jnp.bfloat16
    hbm = pl.BlockSpec(memory_space=pltpu.HBM)
    vmem = pl.BlockSpec(memory_space=pltpu.VMEM)
    dma = pltpu.SemaphoreType.DMA
    code = pl.pallas_call(
        functools.partial(kernel, G, NB, cap, tuple(sizes)),
        out_shape=pltpu.VMEM((n, BINS), bf16),
        in_specs=[hbm] * 5,
        out_specs=vmem,
        scratch_shapes=[
            pltpu.VMEM((n, depth), bf16),
            pltpu.VMEM(projection.shape, bf16),
            pltpu.VMEM((depth, width), bf16),
            pltpu.VMEM((1, width), jnp.int32),
            pltpu.VMEM((1, n), jnp.int32),
            pltpu.VMEM((2, tiles, depth, TILE), bf16),
            pltpu.VMEM((G * cap, n), bf16),
            pltpu.VMEM((G * cap, depth), bf16),
            pltpu.VMEM((H * G * cap, depth), bf16),
            pltpu.VMEM((G * cap, BINS), bf16),
            pltpu.VMEM((max(1, H - 1), G * cap, BINS), bf16),
            pltpu.VMEM((max(1, H - 1), G * cap, BINS), bf16),
            pltpu.VMEM((G * cap, BINS), bf16),
            pltpu.VMEM((G * cap, BINS), bf16),
            dma((5,)),
            dma((C, G - 1)),
            dma((units, max(1, H - 1))),
            dma((tiles,)),
            dma((units, max(1, H - 1))),
            dma((G - 1,)),
            dma((5,)),
        ],
        compiler_params=pltpu.CompilerParams(
            collective_id=0, has_side_effects=True, vmem_limit_bytes=60 * 1024 * 1024),
    )(queries, projection, vectors, bins.reshape(1, -1), routes.reshape(1, -1))
    return logit_scale * decode(code.astype(f32))


def solution(mesh):
    in_specs = (
        P(("parts", "db", "blk"), None),
        P(),
        P(None, ("parts", "db", "blk")),
        P(("parts", "db", "blk")),
        P(("parts", "db", "blk"), None),
    )
    out_specs = P(("parts", "db", "blk"), None)
    return jax.shard_map(
        per_device, mesh=mesh, in_specs=in_specs, out_specs=out_specs, check_vma=False
    )
```

time: 39.8 us -> 35.5 us (0.89)
  Pallas kernels: 38.1 us -> 34.6 us
  other arithmetic: 1.57 us -> 0.76 us
    pallas_call x1, Pallas kernels: 38.1 us -> 34.6 us  [per_device(): pl.pallas_call(functools.partial(kernel, G, NB, cap, tuple(sizes)), out_s...]
    mul x1, other arithmetic: 1.57 us -> 0.76 us  [per_device(): return logit_scale * decode(code.astype(f32))]
where the time goes in v1:
time: 35.5 us; the launch traced here: 35.4 us
  Pallas kernels  34.6 us (97%)
  other arithmetic  0.76 us (2%)
    pallas_call x1, Pallas kernels, per_device(): pl.pallas_call(functools.partial(kernel, G, NB, cap, tuple(sizes)), out_s...  34.6 us
    mul x1, other arithmetic, per_device(): return logit_scale * decode(code.astype(f32))  0.76 us

profile of v1, /device:TPU:0, one launch (start us, length us, event | category | flops | bytes accessed | tf_op | source)
XLA Modules:
  0.0 35.4 jit_solution(479689982609426961)
XLA Ops:
  0.0 34.6 %shard_map.55 = bf16[256,128]{1,0:T(8,128)(2,1)S(1)} custom-call(bf16[256,768]{1,0:T(8,128)(2,1)} %q_hbm.1, bf16[768,768]{1,0:T(8,128)(2,1)} %p_hbm.1, bf16[768,1024]{1,0:T(8,128)(2,1)} %v_hbm.1, s32[1,1024]{1,0:T(1,128)} %bitcast.2, s32[1,256]{1,0:T(1,128)} %bitcast.3), custom_call_target="tpu_custom_call" | custom-call | tf_op jit(solution)/shard_map/pallas_call | solution.py:313
  34.6 0.8 %fusion.3 = f32[256,128]{1,0:T(8,128)} fusion(bf16[256,128]{1,0:T(8,128)(2,1)S(1)} %shard_map.55), kind=kLoop, calls=%fused_computation.6 | loop fusion | flops 229376 | bytes 196608 | tf_op jit(solution)/shard_map/mul | solution.py:344

commit v2 on v1

--- a/solution.py
+++ b/solution.py
@@ -16,6 +16,24 @@
 CODE_SCALE = 2.0 ** 26
 
 
+LEAVE = (
+    (10, 11, 12, 13, 20, 30, 21, 31, 22, 32, 23, 33),
+    (10, 11, 12, 13, 20, 30, 21, 31, 22, 32, 23, 33),
+    (30, 10, 20, 11, 21, 12, 22, 13, 31, 23, 32, 33),
+    (30, 10, 20, 11, 31, 12, 21, 13, 22, 32, 23, 33),
+)
+ARRIVE = (
+    (10, 20, 21, 11, 12, 13, 30, 31, 32, 33, 22, 23),
+    (10, 20, 11, 21, 22, 12, 30, 13, 31, 32, 33, 23),
+    (30, 10, 11, 12, 13, 20, 21, 22, 23, 31, 32, 33),
+    (30, 10, 11, 31, 12, 13, 20, 21, 22, 23, 32, 33),
+)
+LATE = 8
+
+
+LEAST = -3.0e38
+
+
 def encode(score):
     scaled = score * CODE_SCALE
     square = scaled * scaled
@@ -32,8 +50,8 @@
     G, NB, cap, sizes,
     q_hbm, p_hbm, v_hbm, b_hbm, r_hbm,
     out_ref,
-    q_ref, p_ref, raw, bins_ref, routes_ref, slab, chooser, outgoing, rows, own, xout, xin, back, ans,
-    load_sem, z_rs, x_rs, s_rs, xb_rs, zb_rs, sent,
+    q_ref, p_ref, raw, bins_ref, routes_ref, slab, chooser, outgoing, rows, own, xout, xin, back, ans, ans2,
+    load_sem, z_rs, x_rs, s_rs, xb_rs, zb_rs, yb_rs, sent,
 ):
     H = NB // 2
     C = len(sizes)
@@ -46,30 +64,42 @@
 
     load_r = pltpu.make_async_copy(r_hbm, routes_ref, load_sem.at[0])
     load_q = pltpu.make_async_copy(q_hbm, q_ref, load_sem.at[1])
-    load_p = pltpu.make_async_copy(p_hbm, p_ref, load_sem.at[2])
-    load_b = pltpu.make_async_copy(b_hbm, bins_ref, load_sem.at[3])
-    load_v = pltpu.make_async_copy(v_hbm, raw, load_sem.at[4])
-
+    half = depth // 2
+    load_p = [
+        pltpu.make_async_copy(p_hbm.at[pl.ds(i * half, half)], p_ref.at[pl.ds(i * half, half)], load_sem.at[4 + i])
+        for i in range(2)]
+    load_b = pltpu.make_async_copy(b_hbm, bins_ref, load_sem.at[2])
+    load_v = pltpu.make_async_copy(v_hbm, raw, load_sem.at[3])
+    for load in (load_r, load_q, *load_p, load_b):
+        load.start()
+
+    direct = G == 4 and C == 4 and H == 2
+    if direct:
+        ans2[...] = jnp.full(ans2.shape, LEAST, bf16)
     barrier = pltpu.get_barrier_semaphore()
     for o in range(G - 1, 0, -1):
         pl.semaphore_signal(barrier, inc=1, device_id={"db": d ^ o}, device_id_type=MESH)
     for h in range(1, H):
         pl.semaphore_signal(barrier, inc=1, device_id={"blk": k ^ (2 * h)}, device_id_type=MESH)
     pl.semaphore_signal(barrier, inc=1, device_id={"blk": k ^ 1}, device_id_type=MESH)
-    for load in (load_r, load_q, load_p, load_b):
-        load.start()
 
     if G == 4 and C == 4:
-        inner = ((d + 1) // 2) % 2
-        outer_order = [(2, 0), (2, 1), (2, 2), *((1, c) for c in range(C)), *((3, c) for c in range(C)), (2, 3)]
-        inner_order = [(o, c) for o in (1, 2, 3) for c in range(C)]
-
-        def either(a, b):
-            return a if a == b else a + inner * (b - a)
-
-        order = [(either(a, i), either(b, j)) for (a, b), (i, j) in zip(outer_order, inner_order)]
+        inner, odd = ((d + 1) // 2) % 2, k % 2
+
+        def pick4(a, b, c, e):
+            low = a if a == b else a + odd * (b - a)
+            high = c if c == e else c + odd * (e - c)
+            return low if low is high else low + inner * (high - low)
+
+        def orders(*codes):
+            lists = [[divmod(code, 10) for code in one] for one in codes]
+            return [(pick4(*(o for o, _ in at)), pick4(*(c for _, c in at))) for at in zip(*lists, strict=True)]
+
+        leave = orders(*LEAVE)
+        order = orders(*ARRIVE)
         units = [[(0, c) for c in range(C)], order[:4], order[4:8], order[8:10], order[10:]]
     else:
+        leave = [(o, c) for o in range(1, G) for c in range(C)]
         units = [[(o, c) for o in range(G) for c in range(C)]]
     rank = sizes[0]
 
@@ -103,7 +133,7 @@
     def s_copy(t):
         return pltpu.make_async_remote_copy(
             src_ref=slab.at[0, t], dst_ref=slab.at[1, t],
-            send_sem=sent.at[2], recv_sem=s_rs.at[t],
+            send_sem=sent.at[2], recv_sem=s_rs.at[0],
             device_id={"blk": k ^ 1}, device_id_type=MESH)
 
     def xb_copy(u, h):
@@ -117,6 +147,14 @@
             src_ref=back.at[slots(o, c)], dst_ref=ans.at[slots(o, c)],
             send_sem=sent.at[4], recv_sem=zb_rs.at[o - 1],
             device_id={"db": d ^ o}, device_id_type=MESH)
+
+    def yb_copy(u, i):
+        o, c = units[u][i]
+        return pltpu.make_async_remote_copy(
+            src_ref=xout.at[0, pl.ds((sum(len(v) for v in units[:u]) + i) * rank, rank)],
+            dst_ref=ans2.at[slots(o - 2, c)],
+            send_sem=sent.at[3], recv_sem=yb_rs.at[0],
+            device_id={"db": d ^ o, "blk": k ^ 2}, device_id_type=MESH)
 
     def await_bytes(ref, sem):
         pltpu.make_async_copy(ref, ref, sem).wait()
@@ -135,34 +173,35 @@
     slot = jnp.sum(hot * earlier, axis=0, keepdims=True).astype(jnp.int32)
     position = (target ^ d) * cap + slot
 
+    def leave_local():
+        for c in range(C):
+            if H > 1:
+                x_copy(0, 0, c, 0, 1).start()
+
     load_q.wait()
     load_v.start()
-    load_p.wait()
-    projected = jnp.dot(q_ref[...], p_ref[...], preferred_element_type=f32)
+    picks = [
+        jnp.where(
+            lax.broadcasted_iota(jnp.int32, (cap, n), 0) + o * cap == position, 1.0, 0.0
+        ).astype(bf16) for o in range(G)]
+    for o in range(G):
+        chooser[group(o), :] = picks[o]
+    load_p[0].wait()
+    projected = jnp.dot(q_ref[:, :half], p_ref[:half], preferred_element_type=f32)
+    load_p[1].wait()
+    projected += jnp.dot(q_ref[:, half:], p_ref[half:], preferred_element_type=f32)
     normed = (
         projected * lax.rsqrt(jnp.sum(projected * projected, axis=1, keepdims=True) + 1e-06)
     ).astype(bf16)
-
+    chosen = jnp.dot(chooser[...], normed, preferred_element_type=f32).astype(bf16)
+    outgoing[cap:, :] = chosen[cap:]
+    for c in range(C):
+        rows[block(0, c)] = chosen[c * rank:(c + 1) * rank]
     pl.semaphore_wait(barrier, G - 1 + H)
-
-    def choose(o):
-        pick = jnp.where(
-            lax.broadcasted_iota(jnp.int32, (cap, n), 0) + o * cap == position, 1.0, 0.0
-        ).astype(bf16)
-        chooser[group(o), :] = pick
-        chosen = jnp.dot(pick, normed, preferred_element_type=f32).astype(bf16)
-        if o:
-            outgoing[group(o), :] = chosen
-            for c in range(C):
-                z_copy(o, c).start()
-        else:
-            for c in range(C):
-                rows[block(0, c)] = chosen[c * rank:(c + 1) * rank]
-                if H > 1:
-                    x_copy(0, 0, c, 0, 1).start()
-
-    for o in [1, 2, 0, *range(3, G)] if G > 2 else range(G):
-        choose(o)
+    z_copy(*leave[0]).start()
+    leave_local()
+    for o, c in leave[1:]:
+        z_copy(o, c).start()
 
     def relay(u, i):
         o, c = units[u][i]
@@ -207,20 +246,16 @@
                     x_copy(u, o, c, h, step).start()
             step *= 2
 
-    met = [False]
-
     def score(u):
         spread(u)
         for h in range(max(1, H // 2), H):
             await_bytes(whole(u), x_rs.at[u, h - 1])
-        first = not met[0]
-        met[0] = True
+        if u == 0:
+            await_bytes(slab.at[1], s_rs.at[0])
         x = jnp.concatenate([rows[block(o, c, 0, H)] for o, c in units[u]], axis=0)
         best = None
         for side in range(2):
             for t in range(tiles):
-                if first and side == 1:
-                    s_copy(t).wait_recv()
                 sc = jnp.dot(x, slab[side, t], preferred_element_type=f32)
                 top = jnp.maximum(sc[:, :BINS], sc[:, BINS:])
                 best = top if best is None else jnp.maximum(best, top)
@@ -233,12 +268,16 @@
                     own[pl.ds(to + i * rank, rank)] = piece
                 else:
                     xout[h - 1, pl.ds(to + i * rank, rank)] = piece
-        for h in range(1, H):
-            xb_copy(u, h).start()
+        if direct and u >= 3:
+            for i in range(len(units[u])):
+                yb_copy(u, i).start()
+        else:
+            for h in range(1, H):
+                xb_copy(u, h).start()
 
     def combine(u):
         total = own[span(u)]
-        for h in range(1, H):
+        for h in range(1, 1 if direct and u >= 3 else H):
             xb_copy(u, h).wait_recv()
             total = jnp.maximum(total, xin[h - 1, span(u)])
         for i, (o, c) in enumerate(units[u]):
@@ -252,30 +291,51 @@
     def unpick(o):
         if o:
             await_bytes(ans.at[group(o)], zb_rs.at[o - 1])
+        found = ans[group(o)]
+        if direct and o >= 2:
+            found = jnp.maximum(found, ans2[group(o - 2)])
         return lax.dot_general(
-            chooser[group(o), :], ans[group(o)], (((0,), (0,)), ((), ())), preferred_element_type=f32)
+            chooser[group(o), :], found, (((0,), (0,)), ((), ())), preferred_element_type=f32)
 
     if len(units) > 1:
-        for i in range(4):
-            relay(1, i)
-        relay(2, 0)
-        relay(2, 1)
-        score(0)
-        relay(2, 2)
-        relay(2, 3)
-        score(1)
-        combine(0)
-        relay(3, 0)
-        relay(3, 1)
-        relay(4, 0)
-        relay(4, 1)
-        combine(1)
-        score(2)
-        score(3)
-        combine(2)
-        score(4)
-        combine(3)
-        combine(4)
+        def relays(first, last):
+            for p in range(first, last):
+                if p < LATE:
+                    relay(1 + p // 4, p % 4)
+                else:
+                    relay(3 + (p - LATE) // 2, p % 2)
+
+        def finish():
+            score(3)
+            combine(3)
+            combine(2)
+            score(4)
+            combine(4)
+            combine(0)
+
+        @pl.when(inner == 0)
+        def _():
+            relays(0, 4)
+            score(0)
+            relays(4, 8)
+            score(1)
+            relays(8, 11)
+            score(2)
+            relays(11, 12)
+            combine(1)
+            finish()
+
+        @pl.when(inner == 1)
+        def _():
+            relays(0, 4)
+            score(0)
+            relays(4, 7)
+            score(1)
+            relays(7, 10)
+            score(2)
+            relays(10, 12)
+            combine(1)
+            finish()
     else:
         for i, (o, c) in enumerate(units[0]):
             if o:
@@ -283,7 +343,15 @@
         score(0)
         combine(0)
     total = unpick(0)
-    for o in range(1, G):
+    if G > 1:
+        total = total + unpick(1)
+    if direct:
+        late = pick4(*(
+            sum(code // 10 == o for o, at in ((2, 2 - i + j), (3, i + j)) for code in ARRIVE[at][LATE:])
+            for i in (0, 2) for j in (0, 1)))
+        for some in range(2 * C + 1):
+            pl.when(late == some)(lambda some=some: await_bytes(ans2.at[pl.ds(0, some * rank)], yb_rs.at[0]))
+    for o in range(2, G):
         total = total + unpick(o)
     out_ref[...] = total.astype(bf16)
 
@@ -330,12 +398,14 @@
             pltpu.VMEM((max(1, H - 1), G * cap, BINS), bf16),
             pltpu.VMEM((G * cap, BINS), bf16),
             pltpu.VMEM((G * cap, BINS), bf16),
-            dma((5,)),
+            pltpu.VMEM((max(1, G // 2) * cap, BINS), bf16),
+            dma((6,)),
             dma((C, G - 1)),
             dma((units, max(1, H - 1))),
-            dma((tiles,)),
+            dma((1,)),
             dma((units, max(1, H - 1))),
             dma((G - 1,)),
+            dma((1,)),
             dma((5,)),
         ],
         compiler_params=pltpu.CompilerParams(

time: 35.5 us -> 31.7 us (0.89)
  Pallas kernels: 34.6 us -> 30.8 us
    pallas_call x1, Pallas kernels: 34.6 us -> 30.8 us  [per_device(): pl.pallas_call(functools.partial(kernel, G, NB, cap, tuple(sizes)), out_s...]
where the time goes in v2:
time: 31.7 us; the launch traced here: 31.6 us
  Pallas kernels  30.8 us (97%)
  other arithmetic  0.76 us (2%)
    pallas_call x1, Pallas kernels, per_device(): pl.pallas_call(functools.partial(kernel, G, NB, cap, tuple(sizes)), out_s...  30.8 us
    mul x1, other arithmetic, per_device(): return logit_scale * decode(code.astype(f32))  0.76 us

profile of v2, /device:TPU:0, one launch (start us, length us, event | category | flops | bytes accessed | tf_op | source)
XLA Modules:
  0.0 31.6 jit_solution(17414831399501587405)
XLA Ops:
  0.0 30.8 %shard_map.55 = bf16[256,128]{1,0:T(8,128)(2,1)S(1)} custom-call(bf16[256,768]{1,0:T(8,128)(2,1)} %q_hbm.1, bf16[768,768]{1,0:T(8,128)(2,1)} %p_hbm.1, bf16[768,1024]{1,0:T(8,128)(2,1)} %v_hbm.1, s32[1,1024]{1,0:T(1,128)} %bitcast.2, s32[1,256]{1,0:T(1,128)} %bitcast.3), custom_call_target="tpu_custom_call" | custom-call | tf_op jit(solution)/shard_map/pallas_call | solution.py:381
  30.8 0.8 %fusion.3 = f32[256,128]{1,0:T(8,128)} fusion(bf16[256,128]{1,0:T(8,128)(2,1)S(1)} %shard_map.55), kind=kLoop, calls=%fused_computation.6 | loop fusion | flops 229376 | bytes 196608 | tf_op jit(solution)/shard_map/mul | solution.py:414

commit v3 on v2

--- a/solution.py
+++ b/solution.py
@@ -28,7 +28,7 @@
     (30, 10, 11, 12, 13, 20, 21, 22, 23, 31, 32, 33),
     (30, 10, 11, 31, 12, 13, 20, 21, 22, 23, 32, 33),
 )
-LATE = 8
+LATE = (4, 4, 4, 4)
 
 
 LEAST = -3.0e38
@@ -50,7 +50,7 @@
     G, NB, cap, sizes,
     q_hbm, p_hbm, v_hbm, b_hbm, r_hbm,
     out_ref,
-    q_ref, p_ref, raw, bins_ref, routes_ref, slab, chooser, outgoing, rows, own, xout, xin, back, ans, ans2,
+    q_ref, p_ref, raw, bins_ref, routes_ref, slab, chooser, outgoing, rows, own, xout, xin, back, ans, ans2, chooser_t,
     load_sem, z_rs, x_rs, s_rs, xb_rs, zb_rs, yb_rs, sent,
 ):
     H = NB // 2
@@ -152,7 +152,7 @@
         o, c = units[u][i]
         return pltpu.make_async_remote_copy(
             src_ref=xout.at[0, pl.ds((sum(len(v) for v in units[:u]) + i) * rank, rank)],
-            dst_ref=ans2.at[slots(o - 2, c)],
+            dst_ref=ans2.at[slots(o - 1, c)],
             send_sem=sent.at[3], recv_sem=yb_rs.at[0],
             device_id={"db": d ^ o, "blk": k ^ 2}, device_id_type=MESH)
 
@@ -246,7 +246,7 @@
                     x_copy(u, o, c, h, step).start()
             step *= 2
 
-    def score(u):
+    def score(u, straight=False):
         spread(u)
         for h in range(max(1, H // 2), H):
             await_bytes(whole(u), x_rs.at[u, h - 1])
@@ -268,16 +268,19 @@
                     own[pl.ds(to + i * rank, rank)] = piece
                 else:
                     xout[h - 1, pl.ds(to + i * rank, rank)] = piece
-        if direct and u >= 3:
+        if straight and direct:
             for i in range(len(units[u])):
                 yb_copy(u, i).start()
-        else:
-            for h in range(1, H):
-                xb_copy(u, h).start()
-
-    def combine(u):
+        elif len(units) == 1:
+            share(u)
+
+    def share(u):
+        for h in range(1, H):
+            xb_copy(u, h).start()
+
+    def combine(u, straight=False):
         total = own[span(u)]
-        for h in range(1, 1 if direct and u >= 3 else H):
+        for h in range(1, 1 if straight and direct else H):
             xb_copy(u, h).wait_recv()
             total = jnp.maximum(total, xin[h - 1, span(u)])
         for i, (o, c) in enumerate(units[u]):
@@ -288,29 +291,25 @@
                 back[slots(o, c)] = piece
                 zb_copy(o, c).start()
 
-    def unpick(o):
-        if o:
-            await_bytes(ans.at[group(o)], zb_rs.at[o - 1])
-        found = ans[group(o)]
-        if direct and o >= 2:
-            found = jnp.maximum(found, ans2[group(o - 2)])
-        return lax.dot_general(
-            chooser[group(o), :], found, (((0,), (0,)), ((), ())), preferred_element_type=f32)
+    column = jnp.transpose(jnp.broadcast_to(position.astype(f32), (8, n)))[:, :1].astype(jnp.int32)
+    chooser_t[...] = jnp.where(
+        lax.broadcasted_iota(jnp.int32, (n, G * cap), 1) == column, 1.0, 0.0).astype(bf16)
 
     if len(units) > 1:
         def relays(first, last):
             for p in range(first, last):
-                if p < LATE:
+                if p < 8:
                     relay(1 + p // 4, p % 4)
                 else:
-                    relay(3 + (p - LATE) // 2, p % 2)
+                    relay(3 + (p - 8) // 2, p % 2)
 
         def finish():
-            score(3)
-            combine(3)
-            combine(2)
-            score(4)
-            combine(4)
+            score(3, True)
+            combine(3, True)
+            share(0)
+            combine(1)
+            score(4, True)
+            combine(4, True)
             combine(0)
 
         @pl.when(inner == 0)
@@ -319,10 +318,11 @@
             score(0)
             relays(4, 8)
             score(1)
+            share(1)
             relays(8, 11)
-            score(2)
+            score(2, True)
+            combine(2, True)
             relays(11, 12)
-            combine(1)
             finish()
 
         @pl.when(inner == 1)
@@ -331,10 +331,10 @@
             score(0)
             relays(4, 7)
             score(1)
-            relays(7, 10)
-            score(2)
-            relays(10, 12)
-            combine(1)
+            share(1)
+            relays(7, 12)
+            score(2, True)
+            combine(2, True)
             finish()
     else:
         for i, (o, c) in enumerate(units[0]):
@@ -342,17 +342,19 @@
                 relay(0, i)
         score(0)
         combine(0)
-    total = unpick(0)
-    if G > 1:
-        total = total + unpick(1)
+    total = jnp.dot(chooser_t[:, :cap], ans[:cap], preferred_element_type=f32)
+    for o in range(1, G):
+        await_bytes(ans.at[group(o)], zb_rs.at[o - 1])
     if direct:
         late = pick4(*(
-            sum(code // 10 == o for o, at in ((2, 2 - i + j), (3, i + j)) for code in ARRIVE[at][LATE:])
+            sum(code // 10 == o for o, at in ((1, 2 - i + j), (2, 2 - i + j), (3, i + j)) for code in ARRIVE[at][LATE[at]:])
             for i in (0, 2) for j in (0, 1)))
-        for some in range(2 * C + 1):
+        for some in range(3 * C + 1):
             pl.when(late == some)(lambda some=some: await_bytes(ans2.at[pl.ds(0, some * rank)], yb_rs.at[0]))
-    for o in range(2, G):
-        total = total + unpick(o)
+    found = ans[cap:]
+    if direct:
+        found = jnp.maximum(found, ans2[...])
+    total = total + jnp.dot(chooser_t[:, cap:], found, preferred_element_type=f32)
     out_ref[...] = total.astype(bf16)
 
     away = pl.ds(cap, (G - 1) * cap)
@@ -398,7 +400,8 @@
             pltpu.VMEM((max(1, H - 1), G * cap, BINS), bf16),
             pltpu.VMEM((G * cap, BINS), bf16),
             pltpu.VMEM((G * cap, BINS), bf16),
-            pltpu.VMEM((max(1, G // 2) * cap, BINS), bf16),
+            pltpu.VMEM((max(1, G - 1) * cap, BINS), bf16),
+            pltpu.VMEM((n, G * cap), bf16),
             dma((6,)),
             dma((C, G - 1)),
             dma((units, max(1, H - 1))),

time: 31.7 us -> 31.3 us (0.987)
  Pallas kernels: 30.8 us -> 30.4 us
    pallas_call x1, Pallas kernels: 30.8 us -> 30.4 us  [per_device(): pl.pallas_call(functools.partial(kernel, G, NB, cap, tuple(sizes)), out_s...]
where the time goes in v3:
time: 31.3 us; the launch traced here: 31.2 us
  Pallas kernels  30.4 us (97%)
  other arithmetic  0.76 us (2%)
    pallas_call x1, Pallas kernels, per_device(): pl.pallas_call(functools.partial(kernel, G, NB, cap, tuple(sizes)), out_s...  30.4 us
    mul x1, other arithmetic, per_device(): return logit_scale * decode(code.astype(f32))  0.76 us

profile of v3, /device:TPU:0, one launch (start us, length us, event | category | flops | bytes accessed | tf_op | source)
XLA Modules:
  0.0 31.2 jit_solution(13065624671571512125)
XLA Ops:
  0.0 30.4 %shard_map.55 = bf16[256,128]{1,0:T(8,128)(2,1)S(1)} custom-call(bf16[256,768]{1,0:T(8,128)(2,1)} %q_hbm.1, bf16[768,768]{1,0:T(8,128)(2,1)} %p_hbm.1, bf16[768,1024]{1,0:T(8,128)(2,1)} %v_hbm.1, s32[1,1024]{1,0:T(1,128)} %bitcast.2, s32[1,256]{1,0:T(1,128)} %bitcast.3), custom_call_target="tpu_custom_call" | custom-call | tf_op jit(solution)/shard_map/pallas_call | solution.py:383
  30.4 0.8 %fusion.3 = f32[256,128]{1,0:T(8,128)} fusion(bf16[256,128]{1,0:T(8,128)(2,1)S(1)} %shard_map.55), kind=kLoop, calls=%fused_computation.6 | loop fusion | flops 229376 | bytes 196608 | tf_op jit(solution)/shard_map/mul | solution.py:417

commit v4 on v3

--- a/solution.py
+++ b/solution.py
@@ -25,8 +25,8 @@
 ARRIVE = (
     (10, 20, 21, 11, 12, 13, 30, 31, 32, 33, 22, 23),
     (10, 20, 11, 21, 22, 12, 30, 13, 31, 32, 33, 23),
-    (30, 10, 11, 12, 13, 20, 21, 22, 23, 31, 32, 33),
-    (30, 10, 11, 31, 12, 13, 20, 21, 22, 23, 32, 33),
+    (10, 11, 12, 13, 20, 21, 22, 23, 30, 31, 32, 33),
+    (10, 11, 12, 13, 20, 21, 22, 23, 30, 31, 32, 33),
 )
 LATE = (4, 4, 4, 4)
 
@@ -303,11 +303,12 @@
                 else:
                     relay(3 + (p - 8) // 2, p % 2)
 
-        def finish():
+        def finish(last=()):
             score(3, True)
             combine(3, True)
             share(0)
-            combine(1)
+            for u in last:
+                combine(u)
             score(4, True)
             combine(4, True)
             combine(0)
@@ -323,16 +324,20 @@
             score(2, True)
             combine(2, True)
             relays(11, 12)
-            finish()
+            finish((1,))
 
         @pl.when(inner == 1)
         def _():
+            relays(8, 9)
             relays(0, 4)
             score(0)
             relays(4, 7)
             score(1)
             share(1)
-            relays(7, 12)
+            relays(7, 8)
+            relays(9, 10)
+            combine(1)
+            relays(10, 12)
             score(2, True)
             combine(2, True)
             finish()

time: 31.3 us -> 31 us (level)
    pallas_call x1, Pallas kernels: 30.4 us -> 30.1 us  [per_device(): pl.pallas_call(functools.partial(kernel, G, NB, cap, tuple(sizes)), out_s...]
where the time goes in v4:
time: 31 us; the launch traced here: 30.8 us
  Pallas kernels  30.1 us (97%)
  other arithmetic  0.76 us (2%)
    pallas_call x1, Pallas kernels, per_device(): pl.pallas_call(functools.partial(kernel, G, NB, cap, tuple(sizes)), out_s...  30.1 us
    mul x1, other arithmetic, per_device(): return logit_scale * decode(code.astype(f32))  0.76 us

profile of v4, /device:TPU:0, one launch (start us, length us, event | category | flops | bytes accessed | tf_op | source)
XLA Modules:
  0.0 30.8 jit_solution(9606662255077968176)
XLA Ops:
  0.0 30.1 %shard_map.55 = bf16[256,128]{1,0:T(8,128)(2,1)S(1)} custom-call(bf16[256,768]{1,0:T(8,128)(2,1)} %q_hbm.1, bf16[768,768]{1,0:T(8,128)(2,1)} %p_hbm.1, bf16[768,1024]{1,0:T(8,128)(2,1)} %v_hbm.1, s32[1,1024]{1,0:T(1,128)} %bitcast.2, s32[1,256]{1,0:T(1,128)} %bitcast.3), custom_call_target="tpu_custom_call" | custom-call | tf_op jit(solution)/shard_map/pallas_call | solution.py:388
  30.1 0.8 %fusion.3 = f32[256,128]{1,0:T(8,128)} fusion(bf16[256,128]{1,0:T(8,128)(2,1)S(1)} %shard_map.55), kind=kLoop, calls=%fused_computation.6 | loop fusion | flops 229376 | bytes 196608 | tf_op jit(solution)/shard_map/mul | solution.py:422

commit v5 on v4

--- a/solution.py
+++ b/solution.py
@@ -19,7 +19,7 @@
 LEAVE = (
     (10, 11, 12, 13, 20, 30, 21, 31, 22, 32, 23, 33),
     (10, 11, 12, 13, 20, 30, 21, 31, 22, 32, 23, 33),
-    (30, 10, 20, 11, 21, 12, 22, 13, 31, 23, 32, 33),
+    (30, 10, 20, 11, 21, 12, 22, 13, 23, 31, 32, 33),
     (30, 10, 20, 11, 31, 12, 21, 13, 22, 32, 23, 33),
 )
 ARRIVE = (
@@ -179,7 +179,6 @@
                 x_copy(0, 0, c, 0, 1).start()
 
     load_q.wait()
-    load_v.start()
     picks = [
         jnp.where(
             lax.broadcasted_iota(jnp.int32, (cap, n), 0) + o * cap == position, 1.0, 0.0
@@ -189,6 +188,7 @@
     load_p[0].wait()
     projected = jnp.dot(q_ref[:, :half], p_ref[:half], preferred_element_type=f32)
     load_p[1].wait()
+    load_v.start()
     projected += jnp.dot(q_ref[:, half:], p_ref[half:], preferred_element_type=f32)
     normed = (
         projected * lax.rsqrt(jnp.sum(projected * projected, axis=1, keepdims=True) + 1e-06)

time: 31 us -> 31.1 us (level)
  no operation moved by 1% of the time
where the time goes in v5:
time: 31.1 us; the launch traced here: 30.9 us
  Pallas kernels  30.2 us (97%)
  other arithmetic  0.76 us (2%)
    pallas_call x1, Pallas kernels, per_device(): pl.pallas_call(functools.partial(kernel, G, NB, cap, tuple(sizes)), out_s...  30.2 us
    mul x1, other arithmetic, per_device(): return logit_scale * decode(code.astype(f32))  0.76 us

profile of v5, /device:TPU:0, one launch (start us, length us, event | category | flops | bytes accessed | tf_op | source)
XLA Modules:
  0.0 30.9 jit_solution(15829945463134475628)
XLA Ops:
  0.0 30.2 %shard_map.55 = bf16[256,128]{1,0:T(8,128)(2,1)S(1)} custom-call(bf16[256,768]{1,0:T(8,128)(2,1)} %q_hbm.1, bf16[768,768]{1,0:T(8,128)(2,1)} %p_hbm.1, bf16[768,1024]{1,0:T(8,128)(2,1)} %v_hbm.1, s32[1,1024]{1,0:T(1,128)} %bitcast.2, s32[1,256]{1,0:T(1,128)} %bitcast.3), custom_call_target="tpu_custom_call" | custom-call | tf_op jit(solution)/shard_map/pallas_call | solution.py:388
  30.2 0.8 %fusion.3 = f32[256,128]{1,0:T(8,128)} fusion(bf16[256,128]{1,0:T(8,128)(2,1)S(1)} %shard_map.55), kind=kLoop, calls=%fused_computation.6 | loop fusion | flops 229376 | bytes 196608 | tf_op jit(solution)/shard_map/mul | solution.py:422

commit v6 on v5

--- a/solution.py
+++ b/solution.py
@@ -351,10 +351,11 @@
     for o in range(1, G):
         await_bytes(ans.at[group(o)], zb_rs.at[o - 1])
     if direct:
-        late = pick4(*(
+        counts = [
             sum(code // 10 == o for o, at in ((1, 2 - i + j), (2, 2 - i + j), (3, i + j)) for code in ARRIVE[at][LATE[at]:])
-            for i in (0, 2) for j in (0, 1)))
-        for some in range(3 * C + 1):
+            for i in (0, 2) for j in (0, 1)]
+        late = pick4(*counts)
+        for some in sorted(set(counts)):
             pl.when(late == some)(lambda some=some: await_bytes(ans2.at[pl.ds(0, some * rank)], yb_rs.at[0]))
     found = ans[cap:]
     if direct:
@@ -411,7 +412,7 @@
             dma((C, G - 1)),
             dma((units, max(1, H - 1))),
             dma((1,)),
-            dma((units, max(1, H - 1))),
+            dma((min(units, 2), max(1, H - 1))),
             dma((G - 1,)),
             dma((1,)),
             dma((5,)),

time: 31.1 us -> 31.1 us (level)
  no operation moved by 1% of the time
where the time goes in v6:
time: 31.1 us; the launch traced here: 30.9 us
  Pallas kernels  30.2 us (97%)
  other arithmetic  0.76 us (2%)
    pallas_call x1, Pallas kernels, per_device(): pl.pallas_call(functools.partial(kernel, G, NB, cap, tuple(sizes)), out_s...  30.2 us
    mul x1, other arithmetic, per_device(): return logit_scale * decode(code.astype(f32))  0.76 us

profile of v6, /device:TPU:0, one launch (start us, length us, event | category | flops | bytes accessed | tf_op | source)
XLA Modules:
  0.0 30.9 jit_solution(3344338563696069386)
XLA Ops:
  0.0 30.2 %shard_map.55 = bf16[256,128]{1,0:T(8,128)(2,1)S(1)} custom-call(bf16[256,768]{1,0:T(8,128)(2,1)} %q_hbm.1, bf16[768,768]{1,0:T(8,128)(2,1)} %p_hbm.1, bf16[768,1024]{1,0:T(8,128)(2,1)} %v_hbm.1, s32[1,1024]{1,0:T(1,128)} %bitcast.2, s32[1,256]{1,0:T(1,128)} %bitcast.3), custom_call_target="tpu_custom_call" | custom-call | tf_op jit(solution)/shard_map/pallas_call | solution.py:389
  30.2 0.8 %fusion.3 = f32[256,128]{1,0:T(8,128)} fusion(bf16[256,128]{1,0:T(8,128)(2,1)S(1)} %shard_map.55), kind=kLoop, calls=%fused_computation.6 | loop fusion | flops 229376 | bytes 196608 | tf_op jit(solution)/shard_map/mul | solution.py:423
